TPU v7x, 256 devices: a whole 4x4x8 slice. The times are simulated.
256 devices in a mesh: section: 64 (over z, x, core), atlas: 4 (over y).
Axes of the slice: x: 4, y: 4, z: 8, core: 2. Of those that a mesh axis runs over, the one named last changes fastest.
Arguments:
- counts: bfloat16 [131072, 5120], P(('section', 'atlas')), may hold values from -24 to 24
- gene_scale: float32 [5120], replicated, may hold values from 0.3 to 3
- cell_scale: float32 [131072], P(('section', 'atlas')), may hold values from 1 to 48
- gene_basis: bfloat16 [5120, 256], replicated, may hold values from -0.078125 to 0.078125
Outputs:
- cell_basis: bfloat16 [131072, 256], P(('section', 'atlas'))
- gene_side: float32 [5120, 256], P(('section', 'atlas'))
All inputs are finite; a program needn't handle non-finite values.
Results may differ from a plain program's by a relative error of at most 0.0051.
Values sent between devices are 32-bit elements; how exact they have to be, the bound alone decides.
A program may use at most 64 MiB of HBM per device.

v0:
```python
import jax
import jax.numpy as jnp
from jax import lax
from jax.sharding import PartitionSpec as P


def local(counts, gene_scale, cell_scale, gene_basis):
    highest = lax.Precision.HIGHEST
    device_count = lax.axis_size("section") * lax.axis_size("atlas")
    cells_all = counts.shape[0] * device_count
    gene_count = counts.shape[1]
    scaled = (gene_basis.astype(jnp.float32) * gene_scale[:, None]).astype(jnp.bfloat16)
    sketch = jnp.dot(counts, scaled, preferred_element_type=jnp.float32) * cell_scale[:, None]
    weighted = (sketch * cell_scale[:, None]).astype(jnp.bfloat16)
    gene_sums = lax.psum_scatter(
        lax.dot_general(
            counts, weighted, (((0,), (0,)), ((), ())), preferred_element_type=jnp.float32
        ),
        ("section", "atlas"),
        scatter_dimension=0,
        tiled=True,
    )
    gram_local = (
        jnp.dot(sketch.T, sketch, precision=highest, preferred_element_type=jnp.float32) / cells_all
    )
    gram_total = lax.psum(gram_local, ("section", "atlas"))
    lower_factor = jnp.linalg.cholesky(gram_total)
    identity_matrix = jnp.eye(sketch.shape[1], dtype=jnp.float32)
    inverse = jax.scipy.linalg.solve_triangular(lower_factor, identity_matrix, lower=True)
    orthonormal = jnp.dot(sketch, inverse.T, precision=highest, preferred_element_type=jnp.float32)
    cell_basis = orthonormal.astype(jnp.bfloat16)
    rows_mine = gene_count // device_count
    position = lax.axis_index("section") * lax.axis_size("atlas") + lax.axis_index("atlas")
    own_scale = lax.dynamic_slice_in_dim(gene_scale, position * rows_mine, rows_mine)
    rotated = jnp.dot(gene_sums, inverse.T, precision=highest, preferred_element_type=jnp.float32)
    gene_side = rotated * (own_scale / cells_all)[:, None]
    return (cell_basis, gene_side)


def solution(mesh):
    return jax.shard_map(
        local,
        mesh=mesh,
        in_specs=(P(("section", "atlas"), None), P(), P(("section", "atlas")), P()),
        out_specs=(P(("section", "atlas"), None), P(("section", "atlas"), None)),
        check_vma=False,
    )
```

profile of v0, /device:TPU:97, one launch (start us, length us, event | category | flops | bytes accessed | tf_op | source)
XLA Modules:
  0.0 368.3 jit_solution(12759801630752260313)
XLA Ops:
  7.2 0.0 copy-start.1
  7.2 0.0 all-reduce.5.cloned.1.call-start
  7.2 0.0 copy-start
  7.2 5.8 %fusion.2 = f32[256,512]{1,0:T(8,128)S(1)} fusion(bf16[512,5120]{1,0:T(8,128)(2,1)} %param.4, bf16[5120,256]{1,0:T(8,128)(2,1)} %param.7, f32[5120]{0:T(1024)} %param.5, f32[512]{0:T(512)} %param.6), kind=kOutput, calls=%fused_computation.6 | convolution fusion | flops 1346240512 | bytes 8411136 | tf_op jit(solution)/shard_map/dot_general | solution.py:13
  13.0 0.0 copy-done.1
  13.0 0.0 copy-done
  13.0 3.9 %convolution_bitcast_fusion = f32[5120,256]{0,1:T(8,128)} fusion(bf16[512,5120]{1,0:T(8,128)(2,1)S(1)} %copy-done, f32[256,512]{1,0:T(8,128)S(1)} %fusion.2, f32[512]{0:T(512)S(1)} %copy-done.1), kind=kOutput, calls=%fused_computation.2 | convolution fusion | flops 1342439424 | bytes 11012096 | tf_op jit(solution)/shard_map/dot_general | solution.py:16
  16.9 1.3 convolution_multiply_fusion
  18.2 0.0 all-reduce.5.cloned.1.call-update
  18.3 0.8 dynamic-slice_multiply_fusion
  19.1 275.9 %all-reduce.5.cloned.1.call-done = (f32[256,256]{0,1:T(8,128)}, f32[5120,256]{0,1:T(8,128)}) async-done(((f32[256,256]{0,1:T(8,128)}, f32[5120,256]{0,1:T(8,128)}), (f32[256,256]{0,1:T(8,128)}, f32[5120,256]{0,1:T(8,128)})) %all-reduce.5.cloned.1.call-update) | async-done | bytes 5505040 | tf_op jit(solution)/shard_map/psum | solution.py:26
  295.0 1.1 copy.9
  296.1 1.0 fusion.3
  297.1 11.7 %cholesky.50 = f32[128,128]{1,0:T(8,128)S(1)} custom-call(f32[128,128]{1,0:T(8,128)S(1)} %cholesky.118), custom_call_target="Cholesky" | custom-call | tf_op jit(solution)/shard_map/jit(cholesky)/cholesky | solution.py:27
  308.9 9.8 %custom-call.15 = f32[1,128,128]{1,2,0:T(8,128)S(1)} custom-call(f32[1,128,128]{2,1,0:T(8,128)S(1)} %get-tuple-element.25), custom_call_target="InvertDiagBlocksLowerTriangular" | custom-call | tf_op jit(solution)/shard_map/jit(cholesky)/cholesky | solution.py:27
  318.7 0.2 constant_dynamic-update-slice_fusion.1
  318.9 0.3 convolution_subtract_fusion.1
  319.2 11.9 %cholesky.105 = f32[128,128]{1,0:T(8,128)S(1)} custom-call(f32[128,128]{1,0:T(8,128)S(1)} %convolution_subtract_fusion.1), custom_call_target="Cholesky" | custom-call | tf_op jit(solution)/shard_map/jit(cholesky)/cholesky | solution.py:27
  331.1 0.7 compare_reduce_fusion
  333.1 0.1 triangular_solve.63
  333.2 4.0 %while.1 = (s32[]{:T(128)}, f32[256,256]{1,0:T(8,128)S(1)}, s32[2,2]{1,0:T(2,128)S(1)}, f32[2,128,128]{2,1,0:T(8,128)S(1)}, s32[]{:T(128)}) while((s32[]{:T(128)}, f32[256,256]{1,0:T(8,128)S(1)}, s32[2,2]{1,0:T(2,128)S(1)}, f32[2,128,128]{2,1,0:T(8,128)S(1)}, s32[]{:T(128)}) %tuple.27), condition=%wide.while_cond, body=%wide.while_body.sunk | while | flops 2 | bytes 131181 | solution.py:29
  333.2 0.6 fusion.27
  333.8 1.4 bitcast_dynamic-update-slice_fusion.2
  335.2 0.6 fusion.27
  335.8 1.4 bitcast_dynamic-update-slice_fusion.2
  337.2 19.7 %custom-call.16 = f32[2,128,128]{1,2,0:T(8,128)S(1)} custom-call(f32[2,128,128]{2,1,0:T(8,128)S(1)} %get-tuple-element.9), custom_call_target="InvertDiagBlocksLowerTriangular" | custom-call | tf_op jit(solution)/shard_map/jit(_solve_triangular)/triangular_solve | solution.py:29
  356.8 0.3 fusion.6
  357.1 0.3 convolution_subtract_fusion
  357.4 0.3 fusion.9
  357.7 1.7 convolution_convert_fusion
  359.4 2.0 convolution_multiply_fusion.1
  (10 shorter events, 0.2 us)
Async XLA Ops:
  7.2 5.8 %copy-start.1 = (f32[512]{0:T(512)S(1)}, f32[512]{0:T(512)}, u32[]{:S(2)}) copy-start(f32[512]{0:T(512)} %param.6) | copy-start | bytes 6148
  7.2 287.9 %all-reduce.5.cloned.1.call-start = ((), (), s32[]{:S(2)}) async-start(), calls=%async_computation | async-start | bytes 11010048 | tf_op jit(solution)/shard_map/psum | solution.py:26
  7.2 5.8 %copy-start = (bf16[512,5120]{1,0:T(8,128)(2,1)S(1)}, bf16[512,5120]{1,0:T(8,128)(2,1)}, u32[]{:S(2)}) copy-start(bf16[512,5120]{1,0:T(8,128)(2,1)} %param.4) | copy-start | bytes 15728644
Sparse Core Ops, SparseCore 0:
  18.4 276.6 all-reduce.4
where the time goes:
time: 369 us; the launch traced here: 368 us
  waiting for transfers between devices  276 us (75%)
  other arithmetic  55.7 us (15%)
  matrix products  16 us (4%)
  between operations  15.5 us (4%)
  local copies, waits for them, and re-layouts  5.11 us (1%)
    psum x1, waiting for transfers between devices, local(): gram_total = lax.psum(gram_local, ('section', 'atlas'))  276 us
    another operation x6, other arithmetic, local(): lower_factor = jnp.linalg.cholesky(gram_total)  34.1 us
    another operation x3, other arithmetic, local(): jax.scipy.linalg.solve_triangular(lower_factor, identity_matrix, lower=True)  19.7 us
  transfers between devices with their start and end apart: 1, of which 1 were waited for; matrix products, arithmetic and copies ran while one was open for 0% of the time, Pallas kernels for 0%

commit v1 on v0

--- a/solution.py
+++ b/solution.py
@@ -23,7 +23,7 @@
     gram_local = (
         jnp.dot(sketch.T, sketch, precision=highest, preferred_element_type=jnp.float32) / cells_all
     )
-    gram_total = lax.psum(gram_local, ("section", "atlas"))
+    gram_total = lax.psum(lax.psum(gram_local, "section"), "atlas")
     lower_factor = jnp.linalg.cholesky(gram_total)
     identity_matrix = jnp.eye(sketch.shape[1], dtype=jnp.float32)
     inverse = jax.scipy.linalg.solve_triangular(lower_factor, identity_matrix, lower=True)

time: 369 us -> 530 us (1.44)
  waiting for transfers between devices: 276 us -> 435 us
    unnamed x1 -> x4, waiting for transfers between devices: 0.02 us -> 218 us
    psum x1 -> x2, waiting for transfers between devices: 276 us -> 217 us  [local(): gram_total = lax.psum(lax.psum(gram_local, 'section'), 'atlas')]
  transfers between devices with their start and end apart: 1 -> 3, of which waited for: 1 -> 3; matrix products, arithmetic and copies ran while one was open for 0% -> 13% of each run, Pallas kernels for 0% -> 0%
where the time goes in v1:
time: 530 us
  waiting for transfers between devices  435 us (82%)
  other arithmetic  55.5 us (10%)
  matrix products  18.3 us (3%)
  between operations  15.2 us (3%)
    unnamed x4, waiting for transfers between devices  218 us
    psum x2, waiting for transfers between devices, local(): gram_total = lax.psum(lax.psum(gram_local, 'section'), 'atlas')  217 us
    another operation x6, other arithmetic, local(): lower_factor = jnp.linalg.cholesky(gram_total)  34 us
    another operation x3, other arithmetic, local(): jax.scipy.linalg.solve_triangular(lower_factor, identity_matrix, lower=True)  19.7 us
  transfers between devices with their start and end apart: 3, of which 3 were waited for; matrix products, arithmetic and copies ran while one was open for 13% of the time, Pallas kernels for 0%

profile of v1, /device:TPU:97, one launch (start us, length us, event | category | flops | bytes accessed | tf_op | source)
XLA Modules:
  0.0 529.7 jit_solution(5348066120728869532)
XLA Ops:
  7.2 0.0 copy-start
  7.2 0.0 all-reduce.6.cloned.1.call-start
  7.2 5.6 %fusion.2 = f32[256,512]{1,0:T(8,128)S(1)} fusion(bf16[512,5120]{1,0:T(8,128)(2,1)} %param.4, bf16[5120,256]{1,0:T(8,128)(2,1)} %param.7, f32[5120]{0:T(1024)} %param.5, f32[512]{0:T(512)} %param.6), kind=kOutput, calls=%fused_computation.6 | convolution fusion | flops 1346240512 | bytes 8411136 | tf_op jit(solution)/shard_map/dot_general | solution.py:13
  12.8 1.3 convolution_multiply_fusion
  14.2 0.0 all-reduce.6.cloned.1.call-update
  14.2 0.0 all-reduce.8.cloned.1.call-start
  14.2 177.4 %all-reduce.6.cloned.1.call-done = f32[256,256]{0,1:T(8,128)} async-done(((f32[256,256]{0,1:T(8,128)}), f32[256,256]{0,1:T(8,128)}) %all-reduce.6.cloned.1.call-update) | async-done | bytes 262160 | tf_op jit(solution)/shard_map/psum | solution.py:26
  191.6 0.0 all-reduce.8.cloned.1.call-update
  191.7 0.2 all-reduce.10.cloned.1.call-start
  191.9 0.0 copy-done
  191.9 6.4 %convolution_bitcast_fusion = f32[5120,256]{0,1:T(8,128)} fusion(bf16[512,5120]{1,0:T(8,128)(2,1)} %param.4, f32[256,512]{1,0:T(8,128)S(1)} %fusion.2, f32[512]{0:T(512)S(1)} %copy-done), kind=kOutput, calls=%fused_computation.2 | convolution fusion | flops 1342439424 | bytes 11012096 | tf_op jit(solution)/shard_map/dot_general | solution.py:16
  198.3 0.0 all-reduce.10.cloned.1.call-update
  198.4 0.8 dynamic-slice_multiply_fusion
  199.1 39.2 %all-reduce.8.cloned.1.call-done = f32[256,256]{0,1:T(8,128)} async-done(((f32[256,256]{0,1:T(8,128)}), f32[256,256]{0,1:T(8,128)}) %all-reduce.8.cloned.1.call-update) | async-done | bytes 262160 | tf_op jit(solution)/shard_map/psum | solution.py:26
  238.4 1.1 copy.9
  239.5 1.0 fusion.3
  240.5 11.7 %cholesky.50 = f32[128,128]{1,0:T(8,128)S(1)} custom-call(f32[128,128]{1,0:T(8,128)S(1)} %cholesky.118), custom_call_target="Cholesky" | custom-call | tf_op jit(solution)/shard_map/jit(cholesky)/cholesky | solution.py:27
  252.2 9.8 %custom-call.15 = f32[1,128,128]{1,2,0:T(8,128)S(1)} custom-call(f32[1,128,128]{2,1,0:T(8,128)S(1)} %get-tuple-element.23), custom_call_target="InvertDiagBlocksLowerTriangular" | custom-call | tf_op jit(solution)/shard_map/jit(cholesky)/cholesky | solution.py:27
  262.0 0.2 constant_dynamic-update-slice_fusion.1
  262.3 0.3 convolution_subtract_fusion.1
  262.5 11.7 %cholesky.105 = f32[128,128]{1,0:T(8,128)S(1)} custom-call(f32[128,128]{1,0:T(8,128)S(1)} %convolution_subtract_fusion.1), custom_call_target="Cholesky" | custom-call | tf_op jit(solution)/shard_map/jit(cholesky)/cholesky | solution.py:27
  274.3 0.7 compare_reduce_fusion
  276.3 0.1 triangular_solve.63
  276.4 4.2 while.1
  276.6 0.6 fusion.27
  277.2 1.4 bitcast_dynamic-update-slice_fusion.2
  278.6 0.6 fusion.27
  279.2 1.4 bitcast_dynamic-update-slice_fusion.2
  280.6 19.7 %custom-call.16 = f32[2,128,128]{1,2,0:T(8,128)S(1)} custom-call(f32[2,128,128]{2,1,0:T(8,128)S(1)} %get-tuple-element.9), custom_call_target="InvertDiagBlocksLowerTriangular" | custom-call | tf_op jit(solution)/shard_map/jit(_solve_triangular)/triangular_solve | solution.py:29
  300.3 0.3 fusion.6
  300.6 0.3 convolution_subtract_fusion
  300.9 0.3 fusion.9
  301.2 1.7 convolution_convert_fusion
  302.9 218.3 %all-reduce.10.cloned.1.call-done = f32[5120,256]{0,1:T(8,128)} async-done(((f32[5120,256]{0,1:T(8,128)}), f32[5120,256]{0,1:T(8,128)}) %all-reduce.10.cloned.1.call-update) | async-done | bytes 5242896
  521.2 2.0 convolution_multiply_fusion.1
  (10 shorter events, 0.2 us)
Async XLA Ops:
  7.2 184.7 %copy-start = (f32[512]{0:T(512)S(1)}, f32[512]{0:T(512)}, u32[]{:S(2)}) copy-start(f32[512]{0:T(512)} %param.6) | copy-start | bytes 6148
  7.2 184.5 %all-reduce.6.cloned.1.call-start = ((), (), s32[]{:S(2)}) async-start(), calls=%async_computation | async-start | bytes 524288 | tf_op jit(solution)/shard_map/psum | solution.py:26
  14.2 224.2 %all-reduce.8.cloned.1.call-start = ((), (), s32[]{:S(2)}) async-start(), calls=%async_computation.1 | async-start | bytes 524288 | tf_op jit(solution)/shard_map/psum | solution.py:26
  191.7 329.5 %all-reduce.10.cloned.1.call-start = ((), (), s32[]{:S(2)}) async-start(), calls=%async_computation.2 | async-start | bytes 10485760
Sparse Core Ops, SparseCore 0:
  14.3 177.2 all-reduce.5
  193.9 44.3 all-reduce.7
  243.8 277.3 all-reduce.9
